TPU v7x, 512 devices: a whole 4x4x16 slice. The times are simulated.
512 devices in a mesh: row: 4 (over x), col: 128 (over y, z, core).
Axes of the slice: x: 4, y: 4, z: 16, core: 2. Of those that a mesh axis runs over, the one named last changes fastest.
Arguments:
- a_matrix: bfloat16 [4096, 65536], P('row', 'col'), may hold values from -0.0234375 to 0.0234375
- omega: bfloat16 [96, 65536], P(None, 'col'), may hold values from -6 to 6
- col_scale: float32 [65536], P('col'), may hold values from 1 to 48
- cone_point: float32 [4096], P('row'), may hold values from -8 to 8, as said below
- cone_id: int32 [4096], P('row'), may hold values from 0 to 4095, as said below
- cone_kind: int32 [4096], P('row'), may hold values from 0 to 1, as said below
Outputs:
- q_basis: float32 [96, 65536], P(None, 'col')
- r_factor: float32 [96, 96], replicated
Inputs may be any that keep to these rules, and one draw needn't show every extreme that they name: `cone_id`: rows of one cone are consecutive and share one id, the index of the cone's first row; every cone lies inside an aligned block of 4 rows; the last row is a cone of its own. `cone_kind`: 1 marks a second-order cone, 0 nonnegative entries; equal on all rows of a cone; 1 only on cones of two rows or more. `cone_point`: on a second-order cone every non-head entry has magnitude 0.5 or more, and the head's magnitude is at most 0.95 times the norm of the other entries.
All inputs are finite; a program needn't handle non-finite values.
Results may differ from a plain program's by a relative error of at most 0.014.
Values may be sent and summed in bfloat16 or wider, within the bound.
A program may use at most 64 MiB of HBM per device.

v0:
```python
import jax
import jax.numpy as jnp
from jax import lax
from jax.sharding import Mesh
from jax.sharding import PartitionSpec as P

CONE_SPAN = 4
PASSES = 2
COL = ("col_0", "col_1", "col_2")


def sum_in_order(parts, axes, order):
    inside = parts.shape[1:]
    parts = parts.reshape(*(lax.axis_size(a) for a in axes), *inside)
    parts = jnp.moveaxis(parts, order, range(len(axes))).reshape(-1, *inside)
    for k in order:
        parts = lax.psum_scatter(parts, axes[k], scatter_dimension=0, tiled=True)
    return parts[0]


def cut_along(shard, dim, devices):
    lengths = shard.shape
    parts = shard.reshape(*lengths[:dim], devices, lengths[dim] // devices, *lengths[dim + 1 :])
    return jnp.moveaxis(parts, dim, 0)


def summed_rows(shard, axes, order, dim):
    devices = lax.axis_size(axes)
    return sum_in_order(cut_along(shard, dim, devices), axes, order)


def joined_along(parts, dim):
    lengths = list(parts.shape[1:])
    lengths[dim] *= parts.shape[0]
    return jnp.moveaxis(parts, 0, dim).reshape(lengths)


def all_blocks(shard, axes, order):
    parts = shard
    for k in order:
        parts = lax.all_gather(parts, axes[k])
    done = order[::-1]
    back = [done.index(k) for k in range(len(axes))]
    parts = parts.transpose(*back, *range(len(axes), parts.ndim))
    return parts.reshape(-1, *shard.shape)


def gathered_by_axis(shard, axes, order, dim):
    return joined_along(all_blocks(shard, axes, order), dim)


def sent_to_all(shard, axis):
    devices = lax.axis_size(axis)
    return lax.all_to_all(
        jnp.broadcast_to(shard[None], (devices, *shard.shape)), axis, 0, 0, tiled=True
    )


def taken_together(shard, axis):
    return sent_to_all(shard, axis).astype(jnp.float32).sum(axis=0)


def by_axis(shard, axes):
    for axis in axes:
        shard = lax.psum(shard, axis)
    return shard


def cone_operator(cone_vals, cone_ids, cone_types):
    length = cone_vals.shape[0]
    span_len = CONE_SPAN
    blocks = length // span_len
    previous = jnp.concatenate([cone_ids[:1] - 1, cone_ids[:-1]])
    is_head = cone_ids != previous
    second_order = cone_types == 1
    tail_vals = jnp.where(second_order & ~is_head, cone_vals, jnp.float32(0.0))
    block_ids = cone_ids.reshape(blocks, span_len)
    same_cone = (block_ids[:, :, None] == block_ids[:, None, :]).astype(jnp.float32)
    tail_block = tail_vals.reshape(blocks, span_len)
    head_only = jnp.where(is_head, cone_vals, jnp.float32(0.0)).reshape(blocks, span_len)
    tail_sq = jnp.sum(same_cone * (tail_block * tail_block)[:, None, :], axis=2)
    head_vals = jnp.sum(same_cone * head_only[:, None, :], axis=2)
    soc_block = second_order.reshape(blocks, span_len)
    head_block = is_head.reshape(blocks, span_len)
    tail_norm = jnp.sqrt(jnp.where(soc_block, tail_sq, jnp.float32(1.0)))
    cone_ratio = head_vals / tail_norm
    unit_tail = tail_block / tail_norm
    identity_mat = jnp.eye(span_len, dtype=jnp.float32)
    head_rows = 0.5 * (identity_mat[None, :, :] + unit_tail[:, None, :])
    tail_rows = 0.5 * (
        unit_tail[:, :, None] * head_block[:, None, :].astype(jnp.float32)
        + (1.0 + cone_ratio)[:, :, None] * identity_mat[None, :, :]
        - cone_ratio[:, :, None] * unit_tail[:, :, None] * unit_tail[:, None, :]
    )
    soc_rows = jnp.where(head_block[:, :, None], head_rows, tail_rows)
    positive = jnp.where(cone_vals > 0, jnp.float32(1.0), jnp.float32(0.0)).reshape(
        blocks, span_len
    )
    plain_rows = identity_mat[None, :, :] * positive[:, :, None]
    return same_cone * jnp.where(soc_block[:, :, None], soc_rows, plain_rows)


def apply_cones(sketch_rows, operator):
    blocks = operator.shape[0]
    span_len = operator.shape[1]
    width = sketch_rows.shape[0]
    shaped = sketch_rows.reshape(width, blocks, span_len)
    result = jnp.zeros((width, blocks, span_len), jnp.float32)
    for inner in range(span_len):
        result = result + shaped[:, :, inner : inner + 1] * operator[None, :, :, inner]
    return result.reshape(width, blocks * span_len)


def local(a_matrix, omega, col_scale, cone_point, cone_id, cone_kind):
    row_count = a_matrix.shape[0]
    col_count = a_matrix.shape[1]
    total_cols = col_count * lax.axis_size(COL)
    share_rows = row_count // lax.axis_size(COL)
    first_row = lax.axis_index(COL) * share_rows
    operator = cone_operator(
        lax.dynamic_slice_in_dim(cone_point, first_row, share_rows),
        lax.dynamic_slice_in_dim(cone_id, first_row, share_rows),
        lax.dynamic_slice_in_dim(cone_kind, first_row, share_rows),
    )
    vectors = omega
    for repeat in range(PASSES):
        scaled = (vectors.astype(jnp.float32) * col_scale[None, :]).astype(jnp.bfloat16)
        partial_value = lax.dot_general(
            scaled, a_matrix, (((1,), (1,)), ((), ())), preferred_element_type=jnp.float32
        )
        owned = summed_rows(partial_value, COL, (2, 1, 0), 1)
        weighted = apply_cones(owned, operator).astype(jnp.bfloat16)
        back = jnp.dot(
            gathered_by_axis(weighted, COL, (0, 1, 2), 1),
            a_matrix,
            preferred_element_type=jnp.float32,
        )
        summed_back = (
            taken_together(back.astype(jnp.bfloat16), "row").astype(jnp.float32)
            * col_scale[None, :]
        )
        local_gram = jnp.dot(summed_back, summed_back.T, precision=lax.Precision.HIGHEST)
        gram_matrix = by_axis(local_gram, COL) / total_cols
        lower_factor = jnp.linalg.cholesky(gram_matrix)
        orth_basis = lax.linalg.triangular_solve(
            lower_factor, summed_back, left_side=True, lower=True
        )
        vectors = orth_basis.astype(jnp.bfloat16)
    return (orth_basis, lower_factor.T)


def solution(mesh):
    split = Mesh(
        mesh.devices.reshape(mesh.shape["row"], 4, 16, 2), ("row", "col_0", "col_1", "col_2")
    )
    in_specs = (P("row", COL), P(None, COL), P(COL), P("row"), P("row"), P("row"))
    out_specs = (P(None, COL), P())
    return jax.shard_map(local, mesh=split, in_specs=in_specs, out_specs=out_specs, check_vma=False)
```

profile of v0, /device:TPU:1, one launch (start us, length us, event | category | flops | bytes accessed | tf_op | source)
XLA Modules:
  0.0 530.2 jit_solution(10791986055114302990)
XLA Ops:
  7.2 1.2 copy-done
  8.4 1.3 fusion.10
  9.7 0.9 copy.65
  10.7 0.8 dynamic_slice.9
  11.4 0.1 eq.29
  11.6 0.8 broadcast_select_fusion.1
  12.3 0.1 broadcast_in_dim.61
  12.4 0.8 and_select_fusion
  13.2 0.1 reshape.458
  13.3 0.1 broadcast_in_dim.37
  13.4 0.1 mul.340
  13.5 0.1 copy.70
  13.6 0.1 copy.67
  13.7 0.1 copy.69
  13.8 0.1 mul.349
  13.8 0.1 copy.66
  13.9 0.1 fusion.25
  14.0 0.1 copy.68
  14.1 21.8 %reduce-scatter.5.cloned.1.call-done = f32[64,96,8]{1,2,0:T(8,128)} async-done(((f32[128,96,8]{1,2,0:T(8,128)}), f32[64,96,8]{1,2,0:T(8,128)}) %reduce-scatter.5.cloned.1.call-update) | async-done | bytes 196624 | tf_op jit(solution)/shard_map/reduce_scatter | solution.py:17
  36.0 0.1 compare_select_fusion
  36.1 0.1 mul.353
  36.2 0.1 mul.371
  36.3 0.1 mul.365
  36.4 0.1 mul.359
  36.4 1.3 dynamic-slice
  37.7 59.0 %reduce-scatter.7.cloned.1.call-done = f32[4,96,8]{1,2,0:T(8,128)} async-done(((f32[64,96,8]{1,2,0:T(8,128)}), f32[4,96,8]{1,2,0:T(8,128)}) %reduce-scatter.7.cloned.1.call-update) | async-done | bytes 12304 | tf_op jit(solution)/shard_map/reduce_scatter | solution.py:17
  96.7 14.1 %all-reduce = f32[4,96,8]{1,2,0:T(8,128)S(1)} all-reduce(f32[4,96,8]{1,2,0:T(8,128)} %reduce-scatter.7.cloned.1.call-done), channel_id=8, replica_groups=mesh['row'=4,'col_0'=4,'col_1'=16,'col_2'=2] {'col_0'}, use_global_device_ids=true, to_apply=%region_2.3.clone | all-reduce | flops 3072 | bytes 24576
  110.7 0.6 constant_dynamic-slice_fusion.1
  111.5 8.4 %all_gather.32 = bf16[4,96,8]{1,2,0:T(8,128)(2,1)S(1)} all-gather(bf16[1,96,8]{1,2,0:T(8,128)(2,1)S(1)} %add_convert_fusion.1), channel_id=1, replica_groups=mesh['row'=4,'col_0'=4,'col_1'=16,'col_2'=2] {'col_0'}, dimensions={0}, use_global_device_ids=true | all-gather | bytes 7680 | tf_op jit(solution)/shard_map/all_gather | solution.py:41
  120.0 20.8 %all-gather = bf16[64,96,8]{1,2,0:T(8,128)(2,1)S(1)} all-gather(bf16[4,96,8]{1,2,0:T(8,128)(2,1)S(1)} %all_gather.32), channel_id=2, replica_groups=mesh['row'=4,'col_0'=4,'col_1'=16,'col_2'=2] {'col_1'}, dimensions={0}, use_global_device_ids=true | all-gather | bytes 104448 | tf_op jit(solution)/shard_map/all_gather | solution.py:41
  140.8 26.4 %all-gather.1 = bf16[32,4,96,8]{2,3,1,0:T(8,128)(2,1)S(1)} all-gather(bf16[16,4,96,8]{2,3,1,0:T(8,128)(2,1)S(1)} %bitcast.98), channel_id=3, replica_groups=mesh['row'=4,'col_0'=4,'col_1'=16,'col_2'=2] {'col_2'}, dimensions={0}, use_global_device_ids=true | all-gather | bytes 294912 | tf_op jit(solution)/shard_map/all_gather | solution.py:41
  167.3 0.3 convolution_convert_fusion.1
  167.7 11.0 %all_to_all.10 = bf16[4,96,512]{2,1,0:T(8,128)(2,1)S(1)} all-to-all(bf16[4,96,512]{2,1,0:T(8,128)(2,1)S(1)} %broadcast_in_dim.66), channel_id=1, replica_groups=mesh['row'=4,'col_0'=4,'col_1'=16,'col_2'=2] {'row'}, dimensions={0} | all-to-all | bytes 786432 | tf_op jit(solution)/shard_map/all_to_all | solution.py:54
  178.8 0.6 copy-done.1
  179.4 0.3 fusion.8
  179.7 11.2 %psum.42 = f32[96,96]{0,1:T(8,128)S(1)} all-reduce(f32[96,96]{0,1:T(8,128)S(1)} %fusion.8), channel_id=1, replica_groups=mesh['row'=4,'col_0'=4,'col_1'=16,'col_2'=2] {'col_0'}, use_global_device_ids=true, to_apply=%region_6.7 | all-reduce | flops 9216 | bytes 73728 | tf_op jit(solution)/shard_map/psum | solution.py:65
  190.9 40.5 %psum.43 = f32[96,96]{0,1:T(8,128)S(1)} all-reduce(f32[96,96]{0,1:T(8,128)S(1)} %psum.42), channel_id=1, replica_groups=mesh['row'=4,'col_0'=4,'col_1'=16,'col_2'=2] {'col_1'}, use_global_device_ids=true, to_apply=%region_7.8 | all-reduce | flops 9216 | bytes 73728 | tf_op jit(solution)/shard_map/psum | solution.py:65
  231.4 22.6 %psum.44 = f32[96,96]{0,1:T(8,128)S(1)} all-reduce(f32[96,96]{0,1:T(8,128)S(1)} %psum.43), channel_id=1, replica_groups=mesh['row'=4,'col_0'=4,'col_1'=16,'col_2'=2] {'col_2'}, use_global_device_ids=true, to_apply=%region_8.9 | all-reduce | flops 9216 | bytes 73728 | tf_op jit(solution)/shard_map/psum | solution.py:65
  254.1 8.8 %cholesky.44 = f32[96,96]{1,0:T(8,128)S(1)} custom-call(f32[96,96]{1,0:T(8,128)S(1)} %fusion.20), custom_call_target="Cholesky" | custom-call | tf_op jit(solution)/shard_map/jit(cholesky)/cholesky | solution.py:144
  262.9 0.6 compare_reduce_fusion.1
  263.6 0.7 fusion.16
  264.3 7.4 %custom-call.6 = f32[1,96,96]{1,2,0:T(8,128)S(1)} custom-call(f32[1,96,96]{2,1,0:T(8,128)S(1)} %fusion.16), custom_call_target="InvertDiagBlocksLowerTriangular" | custom-call | tf_op jit(solution)/shard_map/triangular_solve/custom-call.0 | solution.py:145
  271.6 0.4 fusion.2
  272.0 0.4 fusion.31
  272.4 0.9 copy.75
  273.4 13.7 %reduce-scatter.9.cloned.1.call-done = f32[64,96,8]{1,2,0:T(8,128)} async-done(((f32[128,96,8]{1,2,0:T(8,128)}), f32[64,96,8]{1,2,0:T(8,128)}) %reduce-scatter.9.cloned.1.call-update) | async-done | bytes 196624 | tf_op jit(solution)/shard_map/reduce_scatter | solution.py:17
  287.1 60.6 %reduce-scatter.11.cloned.1.call-done = f32[4,96,8]{1,2,0:T(8,128)} async-done(((f32[64,96,8]{1,2,0:T(8,128)}), f32[4,96,8]{1,2,0:T(8,128)}) %reduce-scatter.11.cloned.1.call-update) | async-done | bytes 12304 | tf_op jit(solution)/shard_map/reduce_scatter | solution.py:17
  347.6 14.0 %all-reduce.1 = f32[4,96,8]{1,2,0:T(8,128)S(1)} all-reduce(f32[4,96,8]{1,2,0:T(8,128)} %reduce-scatter.11.cloned.1.call-done), channel_id=11, replica_groups=mesh['row'=4,'col_0'=4,'col_1'=16,'col_2'=2] {'col_0'}, use_global_device_ids=true, to_apply=%region_13.16.clone | all-reduce | flops 3072 | bytes 24576
  361.7 0.6 constant_dynamic-slice_fusion
  362.5 8.4 %all_gather.37 = bf16[4,96,8]{1,2,0:T(8,128)(2,1)S(1)} all-gather(bf16[1,96,8]{1,2,0:T(8,128)(2,1)S(1)} %add_convert_fusion), channel_id=1, replica_groups=mesh['row'=4,'col_0'=4,'col_1'=16,'col_2'=2] {'col_0'}, dimensions={0}, use_global_device_ids=true | all-gather | bytes 7680 | tf_op jit(solution)/shard_map/all_gather | solution.py:41
  370.9 20.9 %all-gather.2 = bf16[64,96,8]{1,2,0:T(8,128)(2,1)S(1)} all-gather(bf16[4,96,8]{1,2,0:T(8,128)(2,1)S(1)} %all_gather.37), channel_id=4, replica_groups=mesh['row'=4,'col_0'=4,'col_1'=16,'col_2'=2] {'col_1'}, dimensions={0}, use_global_device_ids=true | all-gather | bytes 104448 | tf_op jit(solution)/shard_map/all_gather | solution.py:41
  391.8 26.4 %all-gather.3 = bf16[32,4,96,8]{2,3,1,0:T(8,128)(2,1)S(1)} all-gather(bf16[16,4,96,8]{2,3,1,0:T(8,128)(2,1)S(1)} %bitcast.99), channel_id=5, replica_groups=mesh['row'=4,'col_0'=4,'col_1'=16,'col_2'=2] {'col_2'}, dimensions={0}, use_global_device_ids=true | all-gather | bytes 294912 | tf_op jit(solution)/shard_map/all_gather | solution.py:41
  418.3 0.3 convolution_convert_fusion
  418.7 10.8 %all_to_all.11 = bf16[4,96,512]{2,1,0:T(8,128)(2,1)S(1)} all-to-all(bf16[4,96,512]{2,1,0:T(8,128)(2,1)S(1)} %broadcast_in_dim.67), channel_id=1, replica_groups=mesh['row'=4,'col_0'=4,'col_1'=16,'col_2'=2] {'row'}, dimensions={0} | all-to-all | bytes 786432 | tf_op jit(solution)/shard_map/all_to_all | solution.py:54
  429.5 0.3 fusion.5
  429.9 11.2 %psum.45 = f32[96,96]{0,1:T(8,128)S(1)} all-reduce(f32[96,96]{0,1:T(8,128)S(1)} %fusion.5), channel_id=1, replica_groups=mesh['row'=4,'col_0'=4,'col_1'=16,'col_2'=2] {'col_0'}, use_global_device_ids=true, to_apply=%region_15.18 | all-reduce | flops 9216 | bytes 73728 | tf_op jit(solution)/shard_map/psum | solution.py:65
  441.1 40.5 %psum.46 = f32[96,96]{0,1:T(8,128)S(1)} all-reduce(f32[96,96]{0,1:T(8,128)S(1)} %psum.45), channel_id=1, replica_groups=mesh['row'=4,'col_0'=4,'col_1'=16,'col_2'=2] {'col_1'}, use_global_device_ids=true, to_apply=%region_16.19 | all-reduce | flops 9216 | bytes 73728 | tf_op jit(solution)/shard_map/psum | solution.py:65
  481.5 22.8 %psum.47 = f32[96,96]{0,1:T(8,128)S(1)} all-reduce(f32[96,96]{0,1:T(8,128)S(1)} %psum.46), channel_id=1, replica_groups=mesh['row'=4,'col_0'=4,'col_1'=16,'col_2'=2] {'col_2'}, use_global_device_ids=true, to_apply=%region_17.20 | all-reduce | flops 9216 | bytes 73728 | tf_op jit(solution)/shard_map/psum | solution.py:65
  504.5 8.8 %cholesky.55 = f32[96,96]{1,0:T(8,128)S(1)} custom-call(f32[96,96]{1,0:T(8,128)S(1)} %fusion.18), custom_call_target="Cholesky" | custom-call | tf_op jit(solution)/shard_map/jit(cholesky)/cholesky | solution.py:144
  513.3 0.6 compare_reduce_fusion
  513.9 0.7 fusion.24
  514.6 0.7 copy.79
  515.3 7.4 %custom-call.7 = f32[1,96,96]{1,2,0:T(8,128)S(1)} custom-call(f32[1,96,96]{2,1,0:T(8,128)S(1)} %get-tuple-element.21), custom_call_target="InvertDiagBlocksLowerTriangular" | custom-call | tf_op jit(solution)/shard_map/triangular_solve/custom-call.0 | solution.py:145
  522.6 1.1 fusion.3
  (41 shorter events, 1.0 us)
Async XLA Ops:
  7.2 1.2 copy-start
  7.2 28.8 %reduce-scatter.5.cloned.1.call-start = ((), (), s32[]{:S(2)}) async-start(), calls=%async_computation.6 | async-start | bytes 786432 | tf_op jit(solution)/shard_map/reduce_scatter | solution.py:17
  10.6 86.1 %reduce-scatter.7.cloned.1.call-start = ((), (), s32[]{:S(2)}) async-start(), calls=%async_computation.7 | async-start | bytes 278528 | tf_op jit(solution)/shard_map/reduce_scatter | solution.py:17
  36.0 251.1 %reduce-scatter.9.cloned.1.call-start = ((), (), s32[]{:S(2)}) async-start(), calls=%async_computation.8 | async-start | bytes 786432 | tf_op jit(solution)/shard_map/reduce_scatter | solution.py:17
  178.7 0.7 copy-start.1
  273.3 74.3 %reduce-scatter.11.cloned.1.call-start = ((), (), s32[]{:S(2)}) async-start(), calls=%async_computation.9 | async-start | bytes 278528 | tf_op jit(solution)/shard_map/reduce_scatter | solution.py:17
Sparse Core Ops, SparseCore 0:
  10.8 25.1 reduce-scatter.4
  38.7 57.8 reduce-scatter.6
  273.4 13.5 reduce-scatter.8
  289.7 57.8 reduce-scatter.10
where the time goes:
time: 531 us; the launch traced here: 530 us
  blocking collectives  310 us (58%)
  waiting for transfers between devices  155 us (29%)
  other arithmetic  37 us (7%)
  between operations  14.1 us (3%)
  local copies, waits for them, and re-layouts  9.2 us (2%)
    reduce_scatter x4, waiting for transfers between devices, sum_in_order(): parts = lax.psum_scatter(parts, axes[k], scatter_dimension=0, tiled=True)  155 us
    psum x6, blocking collectives, by_axis(): shard = lax.psum(shard, axis)  149 us
    all_gather x6, blocking collectives, all_blocks(): parts = lax.all_gather(parts, axes[k])  111 us
    unnamed x2, blocking collectives  28.1 us
    all_to_all x2, blocking collectives, sent_to_all(): lax.all_to_all(jnp.broadcast_to(shard[None], (devices, *shard.shape)), ax...  21.9 us
    another operation x6, other arithmetic, local(): lower_factor = jnp.linalg.cholesky(gram_matrix)  18.9 us
    another operation x3, other arithmetic, local(): lax.linalg.triangular_solve(lower_factor, summed_back, left_side=True, lo...  15.4 us
  transfers between devices with their start and end apart: 4, of which 4 were waited for; matrix products, arithmetic and copies ran while one was open for 1% of the time, Pallas kernels for 0%

commit v1 on v0

v1 whole, which is shorter than its diff:
```python
import jax
import jax.numpy as jnp
from jax import lax
from jax.experimental import pallas as pl
from jax.experimental.pallas import tpu as pltpu
from jax.sharding import Mesh
from jax.sharding import PartitionSpec as P

PASSES = 2
LANES = 128
SUB = 8
COL = ("col_0", "col_1", "col_2")
MESH = pl.DeviceIdType.MESH
HIGHEST = lax.Precision.HIGHEST
NT = (((1,), (1,)), ((), ()))


def offsets_far_first(n):
    return sorted(range(1, n), key=lambda r: -min(r, n - r))


def iota(dim, shape=(SUB, LANES)):
    return lax.broadcasted_iota(jnp.int32, shape, dim)


def factor_and_inverse(gram):
    n = gram.shape[0]
    blocks = n // SUB
    wide = jnp.concatenate([gram, jnp.zeros((n, LANES - n), jnp.float32)], axis=1)
    m = [wide[SUB * i : SUB * (i + 1)] for i in range(blocks)]
    lane, row = iota(1), iota(0)
    upper = [jnp.zeros((SUB, LANES), jnp.float32) for _ in range(blocks)]
    inverse = [jnp.zeros((SUB, LANES), jnp.float32) for _ in range(blocks)]

    def down(block, s):
        return jnp.broadcast_to(block[s : s + 1, :], (SUB, LANES))

    step = 4
    for j in range(0, n, step):
        jb, s0 = j // SUB, j % SUB
        cols = [
            {i: jnp.broadcast_to(m[i][:, j + t : j + t + 1], (SUB, LANES)) for i in range(jb, blocks)}
            for t in range(step)
        ]
        rows = [down(m[jb], s0 + t) for t in range(step)]
        mults, pivots = [], []
        for t in range(step):
            d = down(cols[t][jb], s0 + t)
            inv = 1.0 / d
            root = 1.0 / jnp.sqrt(d)
            at = row == s0 + t
            here = lane == j + t
            upper[jb] = jnp.where(at & (lane >= j + t), rows[t] * root, upper[jb])
            inverse[jb] = jnp.where(at & (lane < j + t), rows[t] * root, jnp.where(at & here, root, inverse[jb]))
            mult = {i: cols[t][i] * inv for i in cols[t]}
            pivot = jnp.where(here, 1.0, rows[t])
            for u in range(t + 1, step):
                rows[u] = jnp.where(here, 0.0, rows[u]) - down(mult[jb], s0 + u) * pivot
                head = down(cols[u][jb], s0 + t)
                cols[u] = {i: cols[u][i] - mult[i] * head for i in cols[u]}
            mults.append(mult)
            pivots.append(jnp.where((lane > j + t) & (lane < j + step), 0.0, pivot))
        inside = (lane >= j) & (lane < j + step)
        for i in range(jb, blocks):
            if i == jb and s0 + step == SUB:
                continue
            new = jnp.where(inside, 0.0, m[i])
            for t in range(step):
                new = new - mults[t][i] * pivots[t]
            m[i] = jnp.where(row >= s0 + step, new, m[i]) if i == jb else new
    return jnp.concatenate(upper, axis=0), jnp.concatenate(inverse, axis=0)


def cone_coefficients(point, ids, kinds):
    width = point.shape[1]

    def ahead(v, d):
        return v if d == 0 else pltpu.roll(v, (-d) % width, 1)

    is_head = jnp.where(ids != ahead(ids, -1), 1.0, 0.0)
    second = jnp.where(kinds == 1, 1.0, 0.0)
    tail = point * second * (1.0 - is_head)
    shifts = range(-3, 4)
    same = {d: jnp.where(ids == ahead(ids, d), 1.0, 0.0) for d in shifts}
    norm_sq = sum(same[d] * ahead(tail * tail, d) for d in shifts)
    head_value = sum(same[d] * ahead(point * is_head, d) for d in shifts)
    norm = jnp.sqrt(jnp.where(second > 0.5, norm_sq, 1.0))
    ratio = head_value / norm
    unit = tail / norm
    positive = jnp.where(point > 0, 1.0, 0.0)
    out = {}
    for d in shifts:
        eye = 1.0 if d == 0 else 0.0
        other_unit, other_head = ahead(unit, d), ahead(is_head, d)
        head_row = 0.5 * (eye + other_unit)
        tail_row = 0.5 * (unit * other_head + (1.0 + ratio) * eye - ratio * unit * other_unit)
        soc = same[d] * jnp.where(is_head > 0.5, head_row, tail_row)
        out[d] = jnp.where(second > 0.5, soc, positive * eye)
    return out


def kernel(
    sizes, omega_hbm, a_hbm, scale_hbm, point_hbm, id_hbm, kind_hbm, q_ref, r_ref,
    omega, a, scale, point, ids, kinds,
    part_out, part_in, cut_out, cut_in, gather_z, chunk_out, weighted, back_out, back_in,
    gram_out, gram_in, gram_z, gram_all,
    load_sem, s_part, r_part, s_cut, r_cut, s_gz, r_gz, s_w, r_w, s_x, r_x, s_ga, r_ga, s_gb, r_gb, s_gc, r_gc,
):
    nx, ny, nz, nc = sizes
    np_ = ny * nc
    sketch, variables = omega.shape
    rows_z = sketch // nz
    rows_p = sketch // np_
    total = variables * ny * nz * nc
    x, y, z, c = (lax.axis_index(n) for n in ("row",) + COL)
    p = y * nc + c

    def on_p(r):
        k = lax.rem(p + r, np_)
        return k, {"col_0": k // nc, "col_2": lax.rem(k, nc)}

    def on_z(r):
        k = lax.rem(z + r, nz)
        return k, {"col_1": k}

    def on_x(r):
        k = lax.rem(x + r, nx)
        return k, {"row": k}

    p_steps, z_steps, x_steps = offsets_far_first(np_), offsets_far_first(nz), offsets_far_first(nx)

    barrier = pltpu.get_barrier_semaphore()
    for on, steps in ((on_z, z_steps), (on_p, p_steps), (on_x, x_steps)):
        for r in steps:
            pl.semaphore_signal(barrier, inc=1, device_id=on(r)[1], device_id_type=MESH)

    loads = [
        pltpu.make_async_copy(src, dst, load_sem.at[k])
        for k, (src, dst) in enumerate(
            ((omega_hbm, omega), (scale_hbm, scale), (a_hbm, a), (point_hbm, point), (id_hbm, ids), (kind_hbm, kinds))
        )
    ]
    for copy in loads:
        copy.start()
    for copy in loads:
        copy.wait()

    def send(src, dst, ss, rs, where):
        copy = pltpu.make_async_remote_copy(
            src_ref=src, dst_ref=dst, send_sem=ss, recv_sem=rs, device_id=where, device_id_type=MESH
        )
        copy.start()
        return copy

    def arrive(dst, ss, rs, where):
        pltpu.make_async_remote_copy(
            src_ref=dst, dst_ref=dst, send_sem=ss, recv_sem=rs, device_id=where, device_id_type=MESH
        ).wait_recv()

    def drain(copies):
        for copy in copies:
            copy.wait_send()

    def sketch_part(scaled, k):
        block = a[pl.ds(pl.multiple_of(k * LANES, LANES), LANES), :]
        return lax.dot_general(scaled, block, NT, preferred_element_type=jnp.float32)

    pl.semaphore_wait(barrier, len(p_steps) + len(z_steps) + len(x_steps))

    coef = None
    pending = []
    scaled = (omega[...].astype(jnp.float32) * scale[...]).astype(jnp.bfloat16)
    first_back = None
    for g in range(PASSES):
        sends = []
        for r in p_steps:
            k, where = on_p(r)
            part_out[g, k] = sketch_part(scaled, k).astype(jnp.bfloat16)
            sends.append(send(part_out.at[g, k], part_in.at[g, p], s_part.at[g, r], r_part.at[g, p], where))
        owned = sketch_part(scaled, p)
        drain(pending)
        gram_sends = []
        if g == 1:
            gram_sends = gram_scatter(0)
        if coef is None:
            coef = cone_coefficients(point[pl.ds(p, 1), :], ids[pl.ds(p, 1), :], kinds[pl.ds(p, 1), :])
        for r in p_steps:
            k, where = on_p(r)
            arrive(part_in.at[g, k], s_part.at[g, r], r_part.at[g, k], where)
            owned = owned + part_in[g, k].astype(jnp.float32)
        for t in range(nz):
            cut_out[g, t] = owned[rows_z * t : rows_z * (t + 1), :].astype(jnp.bfloat16)
        cut_sends = []
        for r in z_steps:
            k, where = on_z(r)
            cut_sends.append(send(cut_out.at[g, k], cut_in.at[g, z], s_cut.at[g, r], r_cut.at[g, z], where))
        drain(sends)
        if g == 1:
            gram_sends = gram_sends + gram_cross(0)
        mine = cut_out[g, z].astype(jnp.float32)
        for r in z_steps[::-1]:
            k, where = on_z(r)
            arrive(cut_in.at[g, k], s_cut.at[g, r], r_cut.at[g, k], where)
            mine = mine + cut_in[g, k].astype(jnp.float32)
        shaped = sum(
            coef[d] * (mine if d == 0 else pltpu.roll(mine, (-d) % LANES, 1)) for d in range(-3, 4)
        )
        gather_z[g, z] = shaped.astype(jnp.bfloat16)
        z_sends = []
        for r in z_steps:
            k, where = on_z(r)
            z_sends.append(send(gather_z.at[g, z], gather_z.at[g, z], s_gz.at[g, r], r_gz.at[g, z], where))
        drain(cut_sends)
        if g == 1:
            gram_sends = gram_sends + gram_spread(0)
        for r in z_steps[::-1]:
            k, where = on_z(r)
            arrive(gather_z.at[g, k], s_gz.at[g, r], r_gz.at[g, k], where)
        chunk = jnp.concatenate([gather_z[g, t].astype(jnp.float32) for t in range(nz)], axis=0).astype(jnp.bfloat16)
        chunk_out[g] = chunk
        w_sends = []
        for r in p_steps:
            k, where = on_p(r)
            w_sends.append(send(chunk_out.at[g], weighted.at[g, p], s_w.at[g, r], r_w.at[g, p], where))
        weighted[g, p] = chunk
        drain(z_sends)
        for r in p_steps:
            k, where = on_p(r)
            arrive(weighted.at[g, k], s_w.at[g, r], r_w.at[g, k], where)
        whole = jnp.concatenate([weighted[g, t] for t in range(np_)], axis=1)
        back = jnp.dot(whole, a[...], preferred_element_type=jnp.float32).astype(jnp.bfloat16)
        back_out[g] = back
        x_sends = []
        for r in x_steps:
            k, where = on_x(r)
            x_sends.append(send(back_out.at[g], back_in.at[g, x], s_x.at[g, r], r_x.at[g, x], where))
        back_in[g, x] = back
        drain(w_sends)
        if g == 1:
            gram = gram_collect(0)
            drain(gram_sends)
            _, inverse = factor_and_inverse(gram)
        for r in x_steps:
            k, where = on_x(r)
            arrive(back_in.at[g, k], s_x.at[g, r], r_x.at[g, k], where)
        pending = x_sends
        summed = back_in[g, 0].astype(jnp.float32)
        for t in range(1, nx):
            summed = summed + back_in[g, t].astype(jnp.float32)
        summed = summed * scale[...]

        def gram_scatter(h):
            local = gram_local[0]
            for t in range(np_):
                gram_out[h, t] = local[rows_p * t : rows_p * (t + 1), :]
            out = []
            for r in p_steps:
                k, where = on_p(r)
                out.append(send(gram_out.at[h, k], gram_in.at[h, p], s_ga.at[h, r], r_ga.at[h, p], where))
            gram_in[h, p] = gram_out[h, p]
            return out

        def gram_cross(h):
            for r in p_steps:
                k, where = on_p(r)
                arrive(gram_in.at[h, k], s_ga.at[h, r], r_ga.at[h, k], where)
            gram_z[h, z] = jnp.sum(gram_in[h], axis=0)
            out = []
            for r in z_steps:
                k, where = on_z(r)
                out.append(send(gram_z.at[h, z], gram_z.at[h, z], s_gb.at[h, r], r_gb.at[h, z], where))
            return out

        def gram_spread(h):
            for r in z_steps[::-1]:
                k, where = on_z(r)
                arrive(gram_z.at[h, k], s_gb.at[h, r], r_gb.at[h, k], where)
            gram_all[h, p] = jnp.sum(gram_z[h], axis=0) / total
            out = []
            for r in p_steps:
                k, where = on_p(r)
                out.append(send(gram_all.at[h, p], gram_all.at[h, p], s_gc.at[h, r], r_gc.at[h, p], where))
            return out

        def gram_collect(h):
            for r in p_steps:
                k, where = on_p(r)
                arrive(gram_all.at[h, k], s_gc.at[h, r], r_gc.at[h, k], where)
            return jnp.concatenate([gram_all[h, t] for t in range(np_)], axis=0)

        if g == 0:
            gram_local = [lax.dot_general(summed, summed, NT, precision=HIGHEST, preferred_element_type=jnp.float32)]
            scaled = (summed * scale[...]).astype(jnp.bfloat16)
        else:
            final = jnp.dot(inverse[:, :sketch], summed, precision=HIGHEST, preferred_element_type=jnp.float32)
            gram_local = [lax.dot_general(final, final, NT, precision=HIGHEST, preferred_element_type=jnp.float32)]
            sends = gram_scatter(1)
            drain(pending)
            sends = sends + gram_cross(1) + gram_spread(1)
            upper, inverse = factor_and_inverse(gram_collect(1))
            q_ref[...] = jnp.dot(inverse[:, :sketch], final, precision=HIGHEST, preferred_element_type=jnp.float32)
            r_ref[...] = upper[:, :sketch]
            drain(sends)


def local(a_matrix, omega, col_scale, cone_point, cone_id, cone_kind):
    sketch, variables = omega.shape
    rows = a_matrix.shape[0]
    nx, ny, nz, nc = (lax.axis_size(n) for n in ("row",) + COL)
    np_ = ny * nc
    g = PASSES
    bf, f32 = jnp.bfloat16, jnp.float32
    dma = pltpu.SemaphoreType.DMA
    any_spec = pl.BlockSpec(memory_space=pl.ANY)
    vmem_spec = pl.BlockSpec(memory_space=pltpu.VMEM)
    per_p, per_z, per_x = dma((g, np_)), dma((g, nz)), dma((g, nx))

    def body(*refs):
        kernel((nx, ny, nz, nc), *refs)

    return tuple(
        pl.pallas_call(
            body,
            out_shape=(
                jax.ShapeDtypeStruct((sketch, variables), f32),
                jax.ShapeDtypeStruct((sketch, sketch), f32),
            ),
            in_specs=[any_spec] * 6,
            out_specs=(vmem_spec, vmem_spec),
            scratch_shapes=[
                pltpu.VMEM((sketch, variables), bf),
                pltpu.VMEM((rows, variables), bf),
                pltpu.VMEM((1, variables), f32),
                pltpu.VMEM((np_, LANES), f32),
                pltpu.VMEM((np_, LANES), jnp.int32),
                pltpu.VMEM((np_, LANES), jnp.int32),
                pltpu.VMEM((g, np_, sketch, LANES), bf),
                pltpu.VMEM((g, np_, sketch, LANES), bf),
                pltpu.VMEM((g, nz, sketch // nz, LANES), bf),
                pltpu.VMEM((g, nz, sketch // nz, LANES), bf),
                pltpu.VMEM((g, nz, sketch // nz, LANES), bf),
                pltpu.VMEM((g, sketch, LANES), bf),
                pltpu.VMEM((g, np_, sketch, LANES), bf),
                pltpu.VMEM((g, sketch, variables), bf),
                pltpu.VMEM((g, nx, sketch, variables), bf),
                pltpu.VMEM((g, np_, sketch // np_, sketch), f32),
                pltpu.VMEM((g, np_, sketch // np_, sketch), f32),
                pltpu.VMEM((g, nz, sketch // np_, sketch), f32),
                pltpu.VMEM((g, np_, sketch // np_, sketch), f32),
                dma((6,)),
                per_p, per_p, per_z, per_z, per_z, per_z, per_p, per_p, per_x, per_x,
                per_p, per_p, per_z, per_z, per_p, per_p,
            ],
            compiler_params=pltpu.CompilerParams(collective_id=0, has_side_effects=True),
        )(
            omega,
            a_matrix,
            col_scale.reshape(1, variables),
            cone_point.reshape(np_, LANES),
            cone_id.reshape(np_, LANES),
            cone_kind.reshape(np_, LANES),
        )
    )


def solution(mesh):
    shape = mesh.shape
    parts = (4, 16, 2) if shape["col"] == 128 else (1, shape["col"], 1)
    split = Mesh(mesh.devices.reshape(shape["row"], *parts), ("row",) + COL)
    in_specs = (P("row", COL), P(None, COL), P(COL), P("row"), P("row"), P("row"))
    out_specs = (P(None, COL), P())
    return jax.shard_map(local, mesh=split, in_specs=in_specs, out_specs=out_specs, check_vma=False)
```

time: 531 us -> 103 us (0.19)
  blocking collectives: 310 us -> 0 us
  waiting for transfers between devices: 155 us -> 0 us
  Pallas kernels: 0 us -> 100 us
  other arithmetic: 37 us -> 0 us
  between operations: 14.1 us -> 0.65 us
  local copies, waits for them, and re-layouts: 9.2 us -> 2.25 us
    reduce_scatter x4 -> x0, waiting for transfers between devices: 155 us -> none  [sum_in_order(): parts = lax.psum_scatter(parts, axes[k], scatter_dimension=0, tiled=True)]
    psum x6 -> x0, blocking collectives: 149 us -> none  [by_axis(): shard = lax.psum(shard, axis)]
    all_gather x6 -> x0, blocking collectives: 111 us -> none  [all_blocks(): parts = lax.all_gather(parts, axes[k])]
    pallas_call x0 -> x1, Pallas kernels: none -> 100 us  [local(): pl.pallas_call(body, out_shape=(jax.ShapeDtypeStruct((sketch, variables),...]
    another operation x9 -> x0, other arithmetic: 34.3 us -> none  [the longest x6 18.9 us: local(): lower_factor = jnp.linalg.cholesky(gram_matrix)]
    unnamed x2 -> x0, blocking collectives: 28.1 us -> none
    all_to_all x2 -> x0, blocking collectives: 21.9 us -> none  [sent_to_all(): lax.all_to_all(jnp.broadcast_to(shard[None], (devices, *shard.shape)), ax...]
  transfers between devices with their start and end apart: 4 -> 0, of which waited for: 4 -> 0; matrix products, arithmetic and copies ran while one was open for 1% -> 0% of each run, Pallas kernels for 0% -> 0%
where the time goes in v1:
time: 103 us
  Pallas kernels  100 us (97%)
  local copies, waits for them, and re-layouts  2.25 us (2%)
    pallas_call x1, Pallas kernels, local(): pl.pallas_call(body, out_shape=(jax.ShapeDtypeStruct((sketch, variables),...  100 us
    unnamed x4, local copies, waits for them, and re-layouts  2.25 us

profile of v1, /device:TPU:1, one launch (start us, length us, event | category | flops | bytes accessed | tf_op | source)
XLA Modules:
  0.0 102.9 jit_solution(6891110874302996243)
XLA Ops:
  0.6 100.0 %shard_map.77 = (f32[96,512]{1,0:T(8,128)}, f32[96,96]{1,0:T(8,128)}) custom-call(bf16[96,512]{1,0:T(8,128)(2,1)} %refs_0_.1, bf16[1024,512]{1,0:T(8,128)(2,1)} %refs_1_.1, f32[1,512]{1,0:T(1,128)} %bitcast.7, f32[8,128]{1,0:T(8,128)} %bitcast.4, s32[8,128]{1,0:T(8,128)} %bitcast.5, s32[8,128]{1,0:T(8,128)} %bitcast.6), custom_call_target="tpu_custom_call" | custom-call | tf_op jit(solution)/shard_map/pallas_call | solution.py:322
  100.7 0.0 copy-start
  100.7 1.6 %copy.10 = f32[96,512]{1,0:T(8,128)} copy(f32[96,512]{1,0:T(8,128)} %get-tuple-element.4) | data formatting | bytes 393216
  102.3 0.0 copy-done
  102.3 0.6 copy.11
Async XLA Ops:
  100.7 1.6 %copy-start = (f32[96,96]{1,0:T(8,128)S(1)}, f32[96,96]{1,0:T(8,128)}, u32[]{:S(2)}) copy-start(f32[96,96]{1,0:T(8,128)} %get-tuple-element.5) | copy-start | bytes 110596

commit v2 on v1

v2 whole, which is shorter than its diff:
```python
import jax
import jax.numpy as jnp
from jax import lax
from jax.experimental import pallas as pl
from jax.experimental.pallas import tpu as pltpu
from jax.sharding import Mesh
from jax.sharding import PartitionSpec as P

PASSES = 2
LANES = 128
SUB = 8
COL = ("col_0", "col_1", "col_2")
MESH = pl.DeviceIdType.MESH
HIGHEST = lax.Precision.HIGHEST
NT = (((1,), (1,)), ((), ()))


def offsets_far_first(n):
    return sorted(range(1, n), key=lambda r: -min(r, n - r))


def iota(dim, shape=(SUB, LANES)):
    return lax.broadcasted_iota(jnp.int32, shape, dim)


class Factor:
    STEP = 4

    def __init__(self, gram):
        self.n = n = gram.shape[0]
        self.blocks = n // SUB
        wide = jnp.concatenate([gram, jnp.zeros((n, LANES - n), jnp.float32)], axis=1)
        self.m = [wide[SUB * i : SUB * (i + 1)] for i in range(self.blocks)]
        self.upper = [jnp.zeros((SUB, LANES), jnp.float32) for _ in range(self.blocks)]
        self.inverse = [jnp.zeros((SUB, LANES), jnp.float32) for _ in range(self.blocks)]

    def run(self, first, last):
        m, upper, inverse, blocks, step = self.m, self.upper, self.inverse, self.blocks, self.STEP
        lane, row = iota(1), iota(0)

        def down(block, s):
            return jnp.broadcast_to(block[s : s + 1, :], (SUB, LANES))

        for j in range(first, last, step):
            jb, s0 = j // SUB, j % SUB
            cols = [
                {i: jnp.broadcast_to(m[i][:, j + t : j + t + 1], (SUB, LANES)) for i in range(jb, blocks)}
                for t in range(step)
            ]
            rows = [down(m[jb], s0 + t) for t in range(step)]
            mults, pivots = [], []
            for t in range(step):
                d = down(cols[t][jb], s0 + t)
                inv = 1.0 / d
                root = 1.0 / jnp.sqrt(d)
                at = row == s0 + t
                here = lane == j + t
                upper[jb] = jnp.where(at & (lane >= j + t), rows[t] * root, upper[jb])
                inverse[jb] = jnp.where(at & (lane < j + t), rows[t] * root, jnp.where(at & here, root, inverse[jb]))
                mult = {i: cols[t][i] * inv for i in cols[t]}
                pivot = jnp.where(here, 1.0, rows[t])
                for u in range(t + 1, step):
                    rows[u] = jnp.where(here, 0.0, rows[u]) - down(mult[jb], s0 + u) * pivot
                    head = down(cols[u][jb], s0 + t)
                    cols[u] = {i: cols[u][i] - mult[i] * head for i in cols[u]}
                mults.append(mult)
                pivots.append(jnp.where((lane > j + t) & (lane < j + step), 0.0, pivot))
            inside = (lane >= j) & (lane < j + step)
            for i in range(jb, blocks):
                if i == jb and s0 + step == SUB:
                    continue
                new = jnp.where(inside, 0.0, m[i])
                for t in range(step):
                    new = new - mults[t][i] * pivots[t]
                m[i] = jnp.where(row >= s0 + step, new, m[i]) if i == jb else new

    def result(self):
        return jnp.concatenate(self.upper, axis=0), jnp.concatenate(self.inverse, axis=0)


def cone_coefficients(point, ids, kinds):
    width = point.shape[1]

    def ahead(v, d):
        return v if d == 0 else pltpu.roll(v, (-d) % width, 1)

    is_head = jnp.where(ids != ahead(ids, -1), 1.0, 0.0)
    second = jnp.where(kinds == 1, 1.0, 0.0)
    tail = point * second * (1.0 - is_head)
    shifts = range(-3, 4)
    same = {d: jnp.where(ids == ahead(ids, d), 1.0, 0.0) for d in shifts}
    norm_sq = sum(same[d] * ahead(tail * tail, d) for d in shifts)
    head_value = sum(same[d] * ahead(point * is_head, d) for d in shifts)
    norm = jnp.sqrt(jnp.where(second > 0.5, norm_sq, 1.0))
    ratio = head_value / norm
    unit = tail / norm
    positive = jnp.where(point > 0, 1.0, 0.0)
    out = {}
    for d in shifts:
        eye = 1.0 if d == 0 else 0.0
        other_unit, other_head = ahead(unit, d), ahead(is_head, d)
        head_row = 0.5 * (eye + other_unit)
        tail_row = 0.5 * (unit * other_head + (1.0 + ratio) * eye - ratio * unit * other_unit)
        soc = same[d] * jnp.where(is_head > 0.5, head_row, tail_row)
        out[d] = jnp.where(second > 0.5, soc, positive * eye)
    return out


def kernel(
    sizes, omega_hbm, a_hbm, scale_hbm, point_hbm, id_hbm, kind_hbm, q_ref, r_ref,
    omega, a, scale, point, ids, kinds,
    part_out, part_in, cut, weighted, near_out, near_in, far_out, far_in,
    gram_out, gram_in, gram_z, gram_all,
    load_sem, a_sem, relay_sem,
    s_part, r_part, s_cut, r_cut, s_w, r_w, s_near, r_near, s_far, r_far, s_ga, r_ga, s_gb, r_gb, s_gc, r_gc,
):
    nx, ny, nz, nc = sizes
    np_ = ny * nc
    ng, nh = 2 * np_, nz // 2
    sketch, variables = omega.shape
    half_k, half_n = sketch // 2, variables // 2
    rows_g = sketch // ng
    total = variables * ny * nz * nc
    x, y, z, c = (lax.axis_index(n) for n in ("row",) + COL)
    p = y * nc + c
    zh, zl = z // 2, lax.rem(z, 2)
    h = p * 2 + zl

    def member(k):
        q = k // 2
        return {"col_0": q // nc, "col_1": zh * 2 + lax.rem(k, 2), "col_2": lax.rem(q, nc)}

    def on_g(r):
        k = lax.rem(h + r, ng)
        return k, member(k)

    def on_h(r):
        k = lax.rem(zh + r, nh)
        return k, {"col_1": k * 2 + zl}

    partners = [{"row": x + 1 - 2 * lax.rem(x, 2)}, {"row": 3 - x}] if nx == 4 else []
    p_steps, g_steps, h_steps = offsets_far_first(np_), offsets_far_first(ng), offsets_far_first(nh)
    near_h = sorted({1, nh - 1}) if nh > 1 else []

    barrier = pltpu.get_barrier_semaphore()
    greet = [on_g(r)[1] for r in g_steps] + [on_h(r)[1] for r in near_h] + partners
    for where in greet:
        pl.semaphore_signal(barrier, inc=1, device_id=where, device_id_type=MESH)

    def a_rows(k):
        return pl.ds(pl.multiple_of(k * LANES, LANES), LANES)

    def load_a(k):
        return pltpu.make_async_copy(a_hbm.at[a_rows(k), :], a.at[a_rows(k), :], a_sem.at[k])

    loads = [
        pltpu.make_async_copy(src, dst, load_sem.at[k])
        for k, (src, dst) in enumerate(
            ((omega_hbm, omega), (scale_hbm, scale), (point_hbm, point), (id_hbm, ids), (kind_hbm, kinds))
        )
    ]
    for copy in loads[:2]:
        copy.start()
    for r in p_steps + [0]:
        load_a(lax.rem(p + r, np_)).start()
    for copy in loads[2:]:
        copy.start()

    def send(src, dst, ss, rs, where):
        copy = pltpu.make_async_remote_copy(
            src_ref=src, dst_ref=dst, send_sem=ss, recv_sem=rs, device_id=where, device_id_type=MESH
        )
        copy.start()
        return copy

    def arrive(dst, ss, rs, where):
        pltpu.make_async_remote_copy(
            src_ref=dst, dst_ref=dst, send_sem=ss, recv_sem=rs, device_id=where, device_id_type=MESH
        ).wait_recv()

    def drain(copies):
        for copy in copies:
            copy.wait_send()

    def sketch_part(scaled, k):
        return lax.dot_general(scaled, a[a_rows(k), :], NT, preferred_element_type=jnp.float32)

    def add_up(ref, g, count):
        out = ref[g, 0].astype(jnp.float32)
        for t in range(1, count):
            out = out + ref[g, t].astype(jnp.float32)
        return out

    def gram_scatter(g, rows):
        local = lax.dot_general(rows, rows, NT, precision=HIGHEST, preferred_element_type=jnp.float32)
        for t in range(ng):
            gram_out[g, t] = local[rows_g * t : rows_g * (t + 1), :]
        out = []
        for r in g_steps:
            k, where = on_g(r)
            out.append(send(gram_out.at[g, k], gram_in.at[g, h], s_ga.at[g, r], r_ga.at[g, h], where))
        gram_in[g, h] = gram_out[g, h]
        return out

    def gram_cross(g):
        for r in g_steps:
            k, where = on_g(r)
            arrive(gram_in.at[g, k], s_ga.at[g, r], r_ga.at[g, k], where)
        gram_z[g, zh] = add_up(gram_in, g, ng)
        out = []
        for r in h_steps:
            k, where = on_h(r)
            out.append(send(gram_z.at[g, zh], gram_z.at[g, zh], s_gb.at[g, r], r_gb.at[g, zh], where))
        return out

    def gram_spread(g):
        for r in h_steps[::-1]:
            k, where = on_h(r)
            arrive(gram_z.at[g, k], s_gb.at[g, r], r_gb.at[g, k], where)
        gram_all[g, h] = add_up(gram_z, g, nh) / total
        out = []
        for r in g_steps:
            k, where = on_g(r)
            out.append(send(gram_all.at[g, h], gram_all.at[g, h], s_gc.at[g, r], r_gc.at[g, h], where))
        return out

    def gram_collect(g):
        for r in g_steps:
            k, where = on_g(r)
            arrive(gram_all.at[g, k], s_gc.at[g, r], r_gc.at[g, k], where)
        return Factor(jnp.concatenate([gram_all[g, t] for t in range(ng)], axis=0))

    pl.semaphore_wait(barrier, len(greet))
    relays = []
    known = 1
    while known < nh // 2:
        relays.append(known)
        known *= 2

    def relay_signal(step):
        for side, r in enumerate((relays[step], nh - relays[step])):
            pl.semaphore_signal(relay_sem.at[step, side], inc=1, device_id=on_h(r)[1], device_id_type=MESH)

    def relay_wait(step):
        for side in range(2):
            pl.semaphore_wait(relay_sem.at[step, side], 1)

    if relays:
        relay_signal(0)
    for copy in loads[:2]:
        copy.wait()
    scaled = (omega[...].astype(jnp.float32) * scale[...]).astype(jnp.bfloat16)
    coef = None
    pending = []
    factor = None
    for g in range(PASSES):
        sends = []
        for r in p_steps + [0]:
            k = lax.rem(p + r, np_)
            if g == 0:
                load_a(k).wait()
            part = sketch_part(scaled, k)
            for t in range(2):
                part_out[g, k, t] = part[half_k * t : half_k * (t + 1)].astype(jnp.bfloat16)
            if r:
                for t in range(2):
                    to = 2 * k + t
                    sends.append(
                        send(part_out.at[g, k, t], part_in.at[g, h], s_part.at[g, to], r_part.at[g, h], member(to))
                    )
            else:
                to = 2 * p + 1 - zl
                sends.append(
                    send(part_out.at[g, p, 1 - zl], part_in.at[g, h], s_part.at[g, to], r_part.at[g, h], member(to))
                )
                owned = jnp.where(zl == 0, part[:half_k], part[half_k:])
        drain(pending)
        gram_sends = []
        if g == 0:
            for step in range(len(relays)):
                relay_wait(step)
                if step + 1 < len(relays):
                    relay_signal(step + 1)
            for copy in loads[2:]:
                copy.wait()
            coef = cone_coefficients(point[pl.ds(p, 1), :], ids[pl.ds(p, 1), :], kinds[pl.ds(p, 1), :])
        else:
            gram_sends = gram_scatter(0, summed)
        for r in g_steps:
            k, where = on_g(r)
            arrive(part_in.at[g, k], s_part.at[g, k], r_part.at[g, k], where)
            owned = owned + part_in[g, k].astype(jnp.float32)
        cut[g, zh] = owned.astype(jnp.bfloat16)
        cut_sends = []
        for r in h_steps:
            k, where = on_h(r)
            cut_sends.append(send(cut.at[g, zh], cut.at[g, zh], s_cut.at[g, r], r_cut.at[g, zh], where))
        drain(sends)
        if g == 1:
            gram_sends = gram_sends + gram_cross(0)
        for r in h_steps[::-1]:
            k, where = on_h(r)
            arrive(cut.at[g, k], s_cut.at[g, r], r_cut.at[g, k], where)
        mine = add_up(cut, g, nh)
        shaped = sum(coef[d] * (mine if d == 0 else pltpu.roll(mine, (-d) % LANES, 1)) for d in range(-3, 4))
        weighted[g, h] = shaped.astype(jnp.bfloat16)
        w_sends = []
        for r in g_steps:
            k, where = on_g(r)
            w_sends.append(send(weighted.at[g, h], weighted.at[g, h], s_w.at[g, r], r_w.at[g, h], where))
        drain(cut_sends)
        if g == 1:
            gram_sends = gram_sends + gram_spread(0)
        for r in g_steps:
            k, where = on_g(r)
            arrive(weighted.at[g, k], s_w.at[g, r], r_w.at[g, k], where)
        whole = jnp.concatenate(
            [jnp.concatenate([weighted[g, 2 * t], weighted[g, 2 * t + 1]], axis=0) for t in range(np_)], axis=1
        )
        near_sends, far_sends = [], []
        for t in range(2):
            back = jnp.dot(whole, a[:, half_n * t : half_n * (t + 1)], preferred_element_type=jnp.float32)
            near_out[g, t] = back.astype(jnp.bfloat16)
            if partners:
                near_sends.append(
                    send(near_out.at[g, t], near_in.at[g, t], s_near.at[g, t], r_near.at[g, t], partners[t])
                )
        drain(w_sends)
        if g == 1:
            factor = gram_collect(0)
            factor.run(0, half_k)
            drain(gram_sends)
        halves = []
        for t in range(2 if partners else 0):
            arrive(near_in.at[g, t], s_near.at[g, t], r_near.at[g, t], partners[t])
            pair = near_out[g, t].astype(jnp.float32) + near_in[g, t].astype(jnp.float32)
            far_out[g, t] = pair.astype(jnp.bfloat16)
            far_sends.append(
                send(far_out.at[g, t], far_in.at[g, t], s_far.at[g, t], r_far.at[g, t], partners[1 - t])
            )
        if g == 1:
            factor.run(half_k, sketch)
        for t in range(2):
            if partners:
                arrive(far_in.at[g, t], s_far.at[g, t], r_far.at[g, t], partners[1 - t])
                halves.append(far_out[g, t].astype(jnp.float32) + far_in[g, t].astype(jnp.float32))
            else:
                halves.append(near_out[g, t].astype(jnp.float32))
        pending = near_sends + far_sends
        summed = jnp.concatenate(halves, axis=1) * scale[...]
        if g == 0:
            scaled = (summed * scale[...]).astype(jnp.bfloat16)
        else:
            _, inverse = factor.result()
            final = jnp.dot(inverse[:, :sketch], summed, precision=HIGHEST, preferred_element_type=jnp.float32)
            sends = gram_scatter(1, final)
            drain(pending)
            sends = sends + gram_cross(1)
            sends = sends + gram_spread(1)
            factor = gram_collect(1)
            factor.run(0, sketch)
            upper, inverse = factor.result()
            q_ref[...] = jnp.dot(inverse[:, :sketch], final, precision=HIGHEST, preferred_element_type=jnp.float32)
            r_ref[...] = upper[:, :sketch]
            drain(sends)


def local(a_matrix, omega, col_scale, cone_point, cone_id, cone_kind):
    sketch, variables = omega.shape
    rows = a_matrix.shape[0]
    nx, ny, nz, nc = (lax.axis_size(n) for n in ("row",) + COL)
    np_ = ny * nc
    ng, nh = 2 * np_, nz // 2
    g = PASSES
    bf, f32, i32 = jnp.bfloat16, jnp.float32, jnp.int32
    dma = pltpu.SemaphoreType.DMA
    any_spec = pl.BlockSpec(memory_space=pl.ANY)
    vmem_spec = pl.BlockSpec(memory_space=pltpu.VMEM)
    per_g, per_h, per_x = dma((g, ng)), dma((g, nh)), dma((g, 2))
    cross = pltpu.VMEM((g, 2, sketch, variables // 2), bf)

    def body(*refs):
        kernel((nx, ny, nz, nc), *refs)

    return tuple(
        pl.pallas_call(
            body,
            out_shape=(
                jax.ShapeDtypeStruct((sketch, variables), f32),
                jax.ShapeDtypeStruct((sketch, sketch), f32),
            ),
            in_specs=[any_spec] * 6,
            out_specs=(vmem_spec, vmem_spec),
            scratch_shapes=[
                pltpu.VMEM((sketch, variables), bf),
                pltpu.VMEM((rows, variables), bf),
                pltpu.VMEM((1, variables), f32),
                pltpu.VMEM((np_, LANES), f32),
                pltpu.VMEM((np_, LANES), i32),
                pltpu.VMEM((np_, LANES), i32),
                pltpu.VMEM((g, np_, 2, sketch // 2, LANES), bf),
                pltpu.VMEM((g, ng, sketch // 2, LANES), bf),
                pltpu.VMEM((g, nh, sketch // 2, LANES), bf),
                pltpu.VMEM((g, ng, sketch // 2, LANES), bf),
                cross, cross, cross, cross,
                pltpu.VMEM((g, ng, sketch // ng, sketch), f32),
                pltpu.VMEM((g, ng, sketch // ng, sketch), f32),
                pltpu.VMEM((g, nh, sketch // ng, sketch), f32),
                pltpu.VMEM((g, ng, sketch // ng, sketch), f32),
                dma((5,)),
                dma((np_,)),
                pltpu.SemaphoreType.REGULAR((3, 2)),
                per_g, per_g, per_h, per_h, per_g, per_g, per_x, per_x, per_x, per_x,
                per_g, per_g, per_h, per_h, per_g, per_g,
            ],
            compiler_params=pltpu.CompilerParams(collective_id=0, has_side_effects=True),
        )(
            omega,
            a_matrix,
            col_scale.reshape(1, variables),
            cone_point.reshape(np_, LANES),
            cone_id.reshape(np_, LANES),
            cone_kind.reshape(np_, LANES),
        )
    )


def solution(mesh):
    shape = mesh.shape
    parts = (4, 16, 2) if shape["col"] == 128 else (1, shape["col"], 1)
    split = Mesh(mesh.devices.reshape(shape["row"], *parts), ("row",) + COL)
    in_specs = (P("row", COL), P(None, COL), P(COL), P("row"), P("row"), P("row"))
    out_specs = (P(None, COL), P())
    return jax.shard_map(local, mesh=split, in_specs=in_specs, out_specs=out_specs, check_vma=False)
```

time: 103 us -> 94.4 us (0.917)
  Pallas kernels: 100 us -> 91.4 us
    pallas_call x1, Pallas kernels: 100 us -> 91.4 us  [local(): pl.pallas_call(body, out_shape=(jax.ShapeDtypeStruct((sketch, variables),...]
where the time goes in v2:
time: 94.4 us; the launch traced here: 94.3 us
  Pallas kernels  91.4 us (97%)
  local copies, waits for them, and re-layouts  2.25 us (2%)
    pallas_call x1, Pallas kernels, local(): pl.pallas_call(body, out_shape=(jax.ShapeDtypeStruct((sketch, variables),...  91.4 us
    unnamed x4, local copies, waits for them, and re-layouts  2.25 us

profile of v2, /device:TPU:1, one launch (start us, length us, event | category | flops | bytes accessed | tf_op | source)
XLA Modules:
  0.0 94.3 jit_solution(11403029358735555840)
XLA Ops:
  0.6 91.4 %shard_map.77 = (f32[96,512]{1,0:T(8,128)}, f32[96,96]{1,0:T(8,128)}) custom-call(bf16[96,512]{1,0:T(8,128)(2,1)} %refs_0_.1, bf16[1024,512]{1,0:T(8,128)(2,1)} %refs_1_.1, f32[1,512]{1,0:T(1,128)} %bitcast.7, f32[8,128]{1,0:T(8,128)} %bitcast.4, s32[8,128]{1,0:T(8,128)} %bitcast.5, s32[8,128]{1,0:T(8,128)} %bitcast.6), custom_call_target="tpu_custom_call" | custom-call | tf_op jit(solution)/shard_map/pallas_call | solution.py:386
  92.0 0.0 copy-start
  92.0 1.6 %copy.10 = f32[96,512]{1,0:T(8,128)} copy(f32[96,512]{1,0:T(8,128)} %get-tuple-element.4) | data formatting | bytes 393216
  93.7 0.0 copy-done
  93.7 0.6 copy.11
Async XLA Ops:
  92.0 1.6 %copy-start = (f32[96,96]{1,0:T(8,128)S(1)}, f32[96,96]{1,0:T(8,128)}, u32[]{:S(2)}) copy-start(f32[96,96]{1,0:T(8,128)} %get-tuple-element.5) | copy-start | bytes 110596

commit v3 on v2

v3 whole, which is shorter than its diff:
```python
import jax
import jax.numpy as jnp
from jax import lax
from jax.experimental import pallas as pl
from jax.experimental.pallas import tpu as pltpu
from jax.sharding import Mesh
from jax.sharding import PartitionSpec as P

PASSES = 2
PIECES = ((0, 16), (16, 32))
LANES = 128
SUB = 8
COL = ("col_0", "col_1", "col_2")
MESH = pl.DeviceIdType.MESH
NT = (((1,), (1,)), ((), ()))


def offsets_far_first(n):
    return sorted(range(1, n), key=lambda r: -min(r, n - r))


def iota(dim, shape=(SUB, LANES)):
    return lax.broadcasted_iota(jnp.int32, shape, dim)


class Factor:
    STEP = 8

    def __init__(self, gram):
        self.n = n = gram.shape[0]
        self.blocks = n // SUB
        self.m = [gram[SUB * i : SUB * (i + 1)] for i in range(self.blocks)]
        self.upper = [jnp.zeros((SUB, LANES), jnp.float32) for _ in range(self.blocks)]
        self.inverse = [jnp.zeros((SUB, LANES), jnp.float32) for _ in range(self.blocks)]

    def run(self, first, last):
        m, upper, inverse, blocks, step = self.m, self.upper, self.inverse, self.blocks, self.STEP
        lane, row = iota(1), iota(0)

        def down(block, s):
            return jnp.broadcast_to(block[s : s + 1, :], (SUB, LANES))

        for j in range(first, last, step):
            jb, s0 = j // SUB, j % SUB
            cols = [
                {i: jnp.broadcast_to(m[i][:, j + t : j + t + 1], (SUB, LANES)) for i in range(jb, blocks)}
                for t in range(step)
            ]
            rows = [down(m[jb], s0 + t) for t in range(step)]
            mults, pivots = [], []
            for t in range(step):
                d = down(cols[t][jb], s0 + t)
                inv = 1.0 / d
                root = lax.rsqrt(d)
                at = row == s0 + t
                here = lane == j + t
                upper[jb] = jnp.where(at & (lane >= j + t), rows[t] * root, upper[jb])
                inverse[jb] = jnp.where(at & (lane < j + t), rows[t] * root, jnp.where(at & here, root, inverse[jb]))
                mult = {i: cols[t][i] * inv for i in cols[t]}
                pivot = jnp.where(here, 1.0, rows[t])
                for u in range(t + 1, step):
                    rows[u] = jnp.where(here, 0.0, rows[u]) - down(mult[jb], s0 + u) * pivot
                    head = down(cols[u][jb], s0 + t)
                    cols[u] = {i: cols[u][i] - mult[i] * head for i in cols[u]}
                mults.append(mult)
                pivots.append(jnp.where((lane > j + t) & (lane < j + step), 0.0, pivot))
            inside = (lane >= j) & (lane < j + step)
            for i in range(jb, blocks):
                if i == jb and s0 + step == SUB:
                    continue
                new = jnp.where(inside, 0.0, m[i])
                for t in range(step):
                    new = new - mults[t][i] * pivots[t]
                m[i] = jnp.where(row >= s0 + step, new, m[i]) if i == jb else new

    def result(self):
        return jnp.concatenate(self.upper, axis=0), jnp.concatenate(self.inverse, axis=0)


def split_dot(left, right):
    f32, bf = jnp.float32, jnp.bfloat16
    lh, rh = left.astype(bf), right.astype(bf)
    ll, rl = (left - lh.astype(f32)).astype(bf), (right - rh.astype(f32)).astype(bf)
    small = jnp.dot(ll, rh, preferred_element_type=f32) + jnp.dot(lh, rl, preferred_element_type=f32)
    return jnp.dot(lh, rh, preferred_element_type=f32) + small


def packed(gram):
    n = gram.shape[0]
    wide = jnp.concatenate([gram, jnp.zeros((n, LANES - n), jnp.float32)], axis=1)
    tiles = [wide[SUB * i : SUB * (i + 1)] for i in range(n // SUB)]
    lane = iota(1)
    out = []
    for i in range(n // SUB // 2):
        cut = SUB * (i + 1)
        out.append(jnp.where(lane < cut, tiles[i], pltpu.roll(tiles[-1 - i], cut, 1)))
    return jnp.concatenate(out, axis=0)


def unpacked(half):
    count = half.shape[0] // SUB
    lane = iota(1)
    low, high = [], []
    for i in range(count):
        tile = half[SUB * i : SUB * (i + 1)]
        cut = SUB * (i + 1)
        low.append(jnp.where(lane < cut, tile, 0.0))
        high.append(jnp.where(lane < SUB * (2 * count - i), pltpu.roll(tile, LANES - cut, 1), 0.0))
    n = 2 * count * SUB
    lower = jnp.concatenate(low + high[::-1] + [jnp.zeros((LANES - n, LANES), jnp.float32)], axis=0)
    row, col = iota(0, (LANES, LANES)), iota(1, (LANES, LANES))
    return jnp.where(col // SUB > row // SUB, lower.T, lower)[:n]


def cone_coefficients(point, ids, kinds):
    width = point.shape[1]

    def ahead(v, d):
        return v if d == 0 else pltpu.roll(v, (-d) % width, 1)

    is_head = jnp.where(ids != ahead(ids, -1), 1.0, 0.0)
    second = jnp.where(kinds == 1, 1.0, 0.0)
    tail = point * second * (1.0 - is_head)
    shifts = range(-3, 4)
    same = {d: jnp.where(ids == ahead(ids, d), 1.0, 0.0) for d in shifts}
    norm_sq = sum(same[d] * ahead(tail * tail, d) for d in shifts)
    head_value = sum(same[d] * ahead(point * is_head, d) for d in shifts)
    norm = jnp.sqrt(jnp.where(second > 0.5, norm_sq, 1.0))
    ratio = head_value / norm
    unit = tail / norm
    positive = jnp.where(point > 0, 1.0, 0.0)
    out = {}
    for d in shifts:
        eye = 1.0 if d == 0 else 0.0
        other_unit, other_head = ahead(unit, d), ahead(is_head, d)
        head_row = 0.5 * (eye + other_unit)
        tail_row = 0.5 * (unit * other_head + (1.0 + ratio) * eye - ratio * unit * other_unit)
        soc = same[d] * jnp.where(is_head > 0.5, head_row, tail_row)
        out[d] = jnp.where(second > 0.5, soc, positive * eye)
    return out


def kernel(
    sizes, omega_hbm, a_hbm, scale_hbm, point_hbm, id_hbm, kind_hbm, q_ref, r_ref,
    omega, a, scale, point, ids, kinds,
    part_out, part_in, cut, weighted, near_out, near_in, far_out, far_in,
    gram_g, gram_h,
    load_sem, a_sem, relay_sem,
    s_part, r_part, s_cut, r_cut, s_w, r_w, s_near, r_near, s_far, r_far, s_ga, r_ga, s_gb, r_gb,
):
    nx, ny, nz, nc = sizes
    np_ = ny * nc
    ng, nh = 2 * np_, nz // 2
    sketch, variables = omega.shape
    half_k, half_n = sketch // 2, variables // 2
    total = variables * ny * nz * nc
    x, y, z, c = (lax.axis_index(n) for n in ("row",) + COL)
    p = y * nc + c
    zh, zl = z // 2, lax.rem(z, 2)
    h = p * 2 + zl
    ys = [y] + [lax.rem(y + r, ny) for r in range(1, ny)]
    cs = [c, 1 - c] if nc == 2 else [c]
    zls = [zl, 1 - zl]
    zhs = [zh] + [lax.rem(zh + r, nh) for r in range(1, nh)]

    def on_g(r):
        ry, rc, rz = r
        where = {"col_0": ys[ry], "col_1": zh * 2 + zls[rz], "col_2": cs[rc]}
        return (ys[ry] * nc + cs[rc]) * 2 + zls[rz], where

    def on_h(r):
        return zhs[r], {"col_1": zhs[r] * 2 + zl}

    partners = [{"row": x + 1 - 2 * lax.rem(x, 2)}, {"row": 3 - x}] if nx == 4 else []
    y_steps = offsets_far_first(ny) + [0]
    g_steps = [(ry, rc, rz) for ry in y_steps for rc in range(nc) for rz in (1, 0) if ry or rc or rz]
    h_steps = offsets_far_first(nh)
    near_h = sorted({1, nh - 1}) if nh > 1 else []

    barrier = pltpu.get_barrier_semaphore()
    def a_rows(k):
        return pl.ds(pl.multiple_of(k * nc * LANES, nc * LANES), nc * LANES)

    def load_a(k):
        return pltpu.make_async_copy(a_hbm.at[a_rows(k), :], a.at[a_rows(k), :], a_sem.at[k])

    loads = [
        pltpu.make_async_copy(src, dst, load_sem.at[k])
        for k, (src, dst) in enumerate(
            ((omega_hbm, omega), (scale_hbm, scale), (point_hbm, point), (id_hbm, ids), (kind_hbm, kinds))
        )
    ]
    for copy in loads[:2]:
        copy.start()
    for r in y_steps:
        load_a(ys[r]).start()
    for copy in loads[2:]:
        copy.start()
    greet = [on_g(r)[1] for r in g_steps] + [on_h(r)[1] for r in near_h] + partners
    for where in greet:
        pl.semaphore_signal(barrier, inc=1, device_id=where, device_id_type=MESH)


    def send(src, dst, ss, rs, where):
        copy = pltpu.make_async_remote_copy(
            src_ref=src, dst_ref=dst, send_sem=ss, recv_sem=rs, device_id=where, device_id_type=MESH
        )
        copy.start()
        return copy

    def arrive(dst, ss, rs, where):
        pltpu.make_async_remote_copy(
            src_ref=dst, dst_ref=dst, send_sem=ss, recv_sem=rs, device_id=where, device_id_type=MESH
        ).wait_recv()

    def drain(copies):
        for copy in copies:
            copy.wait_send()

    def sketch_part(scaled, k):
        return lax.dot_general(scaled, a[a_rows(k), :], NT, preferred_element_type=jnp.float32)

    def add_up(ref, g, count, piece=(0, half_k)):
        lo, hi = piece[0], piece[0] + piece[1]
        out = ref[g, 0, lo:hi].astype(jnp.float32)
        for t in range(1, count):
            out = out + ref[g, t, lo:hi].astype(jnp.float32)
        return out

    def gram_start(g, rows):
        rows = rows.astype(jnp.bfloat16)
        local = lax.dot_general(rows, rows, NT, preferred_element_type=jnp.float32)
        gram_g[g, h] = packed(local).astype(jnp.bfloat16)
        out = []
        for r in g_steps:
            k, where = on_g(r)
            out.append(send(gram_g.at[g, h], gram_g.at[g, h], s_ga.at[g, k], r_ga.at[g, h], where))
        return out

    def gram_cross(g):
        for r in g_steps:
            k, where = on_g(r)
            arrive(gram_g.at[g, k], s_ga.at[g, k], r_ga.at[g, k], where)
        gram_h[g, zh] = add_up(gram_g, g, ng).astype(jnp.bfloat16)
        out = []
        for r in h_steps:
            k, where = on_h(r)
            out.append(send(gram_h.at[g, zh], gram_h.at[g, zh], s_gb.at[g, r], r_gb.at[g, zh], where))
        return out

    def gram_collect(g):
        for r in h_steps[::-1]:
            k, where = on_h(r)
            arrive(gram_h.at[g, k], s_gb.at[g, r], r_gb.at[g, k], where)
        return Factor(unpacked(add_up(gram_h, g, nh) / total))

    relays = []
    known = 1
    while known < nh // 2:
        relays.append(known)
        known *= 2

    def relay_signal(step):
        for side, r in enumerate((relays[step], nh - relays[step])):
            pl.semaphore_signal(relay_sem.at[step, side], inc=1, device_id=on_h(r)[1], device_id_type=MESH)

    def relay_wait(step):
        for side in range(2):
            pl.semaphore_wait(relay_sem.at[step, side], 1)

    def view(ref, index, piece):
        return ref.at[(*index, pl.ds(piece[0], piece[1]))]

    count = len(PIECES)

    def store_part(g, k, part, pieces):
        for e in range(nc):
            at = 0
            for lo, n in pieces:
                for t in range(2):
                    rows = part[at : at + n, LANES * e : LANES * (e + 1)]
                    part_out[g, k * nc + e, t, lo : lo + n] = rows.astype(jnp.bfloat16)
                    at += n

    def send_part(g, i, r):
        out = []
        for rc in range(nc):
            for rz in (1, 0):
                if r or rc or rz:
                    to, where = on_g((r, rc, rz))
                    out.append(
                        send(
                            view(part_out, (g, ys[r] * nc + cs[rc], zls[rz]), PIECES[i]),
                            view(part_in, (g, h), PIECES[i]),
                            s_part.at[g, i, to], r_part.at[g, i, h], where,
                        )
                    )
        return out

    def own_rows(part, at, n):
        mine = jnp.where(c == 0, part[at : at + 2 * n, :LANES], part[at : at + 2 * n, -LANES:])
        return jnp.where(zl == 0, mine[:n], mine[n:])

    for copy in loads[:2]:
        copy.wait()
    scaled = (omega[...].astype(jnp.float32) * scale[...]).astype(jnp.bfloat16)
    scaled = jnp.concatenate(
        [scaled[half_k * t + lo : half_k * t + lo + n] for lo, n in PIECES for t in range(2)], axis=0
    )
    sends, owned = [], []
    for r in y_steps:
        load_a(ys[r]).wait()
        part = sketch_part(scaled, ys[r])
        store_part(0, ys[r], part, PIECES)
    at = 0
    for lo, n in PIECES:
        owned.append(own_rows(part, at, n))
        at += 2 * n
    pl.semaphore_wait(barrier, len(greet))
    if relays:
        relay_signal(0)
    for i in range(count):
        for r in y_steps:
            sends += send_part(0, i, r)
    for step in range(len(relays)):
        relay_wait(step)
        if step + 1 < len(relays):
            relay_signal(step + 1)
    for copy in loads[2:]:
        copy.wait()
    coef = cone_coefficients(point[pl.ds(p, 1), :], ids[pl.ds(p, 1), :], kinds[pl.ds(p, 1), :])
    gram_sends, late = [], []
    for g in range(PASSES):
        cut_sends = []
        for i, piece in enumerate(PIECES):
            lo, n = piece
            mine = owned[i]
            for r in g_steps:
                k, where = on_g(r)
                arrive(view(part_in, (g, k), piece), s_part.at[g, i, k], r_part.at[g, i, k], where)
                mine = mine + part_in[g, k, lo : lo + n].astype(jnp.float32)
            cut[g, zh, lo : lo + n] = mine.astype(jnp.bfloat16)
            for r in h_steps:
                k, where = on_h(r)
                cut_sends.append(
                    send(
                        view(cut, (g, zh), piece), view(cut, (g, zh), piece),
                        s_cut.at[g, i, r], r_cut.at[g, i, zh], where,
                    )
                )
        drain(sends)
        drain(late)
        if g == 1:
            gram_sends += gram_cross(0)
        w_sends = []
        for i, piece in enumerate(PIECES):
            lo, n = piece
            for r in h_steps[::-1]:
                k, where = on_h(r)
                arrive(view(cut, (g, k), piece), s_cut.at[g, i, r], r_cut.at[g, i, k], where)
            mine = add_up(cut, g, nh, piece)
            shaped = sum(coef[d] * (mine if d == 0 else pltpu.roll(mine, (-d) % LANES, 1)) for d in range(-3, 4))
            weighted[g, h, lo : lo + n] = shaped.astype(jnp.bfloat16)
            for r in g_steps:
                k, where = on_g(r)
                w_sends.append(
                    send(
                        view(weighted, (g, h), piece), view(weighted, (g, h), piece),
                        s_w.at[g, i, k], r_w.at[g, i, h], where,
                    )
                )
        drain(cut_sends)
        near_sends, far_sends = [], []
        for i, piece in enumerate(PIECES):
            lo, n = piece
            for r in g_steps:
                k, where = on_g(r)
                arrive(view(weighted, (g, k), piece), s_w.at[g, i, k], r_w.at[g, i, k], where)
            whole = jnp.concatenate(
                [
                    jnp.concatenate([weighted[g, 2 * t, lo : lo + n], weighted[g, 2 * t + 1, lo : lo + n]], axis=0)
                    for t in range(np_)
                ],
                axis=1,
            )
            for t in range(2):
                back = jnp.dot(whole, a[:, half_n * t : half_n * (t + 1)], preferred_element_type=jnp.float32)
                near_out[g, t, 2 * lo : 2 * (lo + n)] = back.astype(jnp.bfloat16)
                if partners:
                    double = (2 * lo, 2 * n)
                    near_sends.append(
                        send(
                            view(near_out, (g, t), double), view(near_in, (g, t), double),
                            s_near.at[g, i, t], r_near.at[g, i, t], partners[t],
                        )
                    )
        drain(w_sends)
        if g == 1:
            factor = gram_collect(0)
            factor.run(0, 24)
        for i, piece in enumerate(PIECES if partners else ()):
            double = (2 * piece[0], 2 * piece[1])
            lo, hi = double[0], double[0] + double[1]
            for t in range(2):
                arrive(view(near_in, (g, t), double), s_near.at[g, i, t], r_near.at[g, i, t], partners[t])
                pair = near_out[g, t, lo:hi].astype(jnp.float32) + near_in[g, t, lo:hi].astype(jnp.float32)
                far_out[g, t, lo:hi] = pair.astype(jnp.bfloat16)
                far_sends.append(
                    send(
                        view(far_out, (g, t), double), view(far_in, (g, t), double),
                        s_far.at[g, i, t], r_far.at[g, i, t], partners[1 - t],
                    )
                )
            if g == 1 and i == 0:
                factor.run(24, half_k)
        if g == 1:
            factor.run(half_k, sketch)
            drain(gram_sends)
        late = near_sends + far_sends
        summed, owned, sends = [], [], []
        for i, piece in enumerate(PIECES):
            double = (2 * piece[0], 2 * piece[1])
            lo, hi = double[0], double[0] + double[1]
            halves = []
            for t in range(2):
                if partners:
                    arrive(view(far_in, (g, t), double), s_far.at[g, i, t], r_far.at[g, i, t], partners[1 - t])
                    halves.append(far_out[g, t, lo:hi].astype(jnp.float32) + far_in[g, t, lo:hi].astype(jnp.float32))
                else:
                    halves.append(near_out[g, t, lo:hi].astype(jnp.float32))
            rows = jnp.concatenate(halves, axis=1) * scale[...]
            summed.append(rows)
            if g == 0:
                scaled = (rows * scale[...]).astype(jnp.bfloat16)
                for r in y_steps:
                    part = sketch_part(scaled, ys[r])
                    store_part(1, ys[r], part, (piece,))
                    sends += send_part(1, i, r)
                owned.append(own_rows(part, 0, piece[1]))
        summed = jnp.concatenate([v[n * t : n * (t + 1)] for t in range(2) for v, (_, n) in zip(summed, PIECES)], axis=0)
        if g == 0:
            gram_sends += gram_start(0, summed)
        else:
            _, inverse = factor.result()
            final = split_dot(inverse[:, :sketch], summed)
            sends = gram_start(1, final)
            drain(late)
            sends += gram_cross(1)
            factor = gram_collect(1)
            factor.run(0, sketch)
            upper, inverse = factor.result()
            q_ref[...] = split_dot(inverse[:, :sketch], final)
            r_ref[...] = upper[:, :sketch]
            drain(sends)


def local(a_matrix, omega, col_scale, cone_point, cone_id, cone_kind):
    sketch, variables = omega.shape
    rows = a_matrix.shape[0]
    nx, ny, nz, nc = (lax.axis_size(n) for n in ("row",) + COL)
    np_ = ny * nc
    ng, nh = 2 * np_, nz // 2
    g = PASSES
    bf, f32, i32 = jnp.bfloat16, jnp.float32, jnp.int32
    dma = pltpu.SemaphoreType.DMA
    any_spec = pl.BlockSpec(memory_space=pl.ANY)
    vmem_spec = pl.BlockSpec(memory_space=pltpu.VMEM)
    n = len(PIECES)
    per_g, per_h, per_x = dma((g, n, ng)), dma((g, n, nh)), dma((g, n, 2))
    gram_by_g, gram_by_h = dma((g, ng)), dma((g, nh))
    cross = pltpu.VMEM((g, 2, sketch, variables // 2), bf)

    def body(*refs):
        kernel((nx, ny, nz, nc), *refs)

    return tuple(
        pl.pallas_call(
            body,
            out_shape=(
                jax.ShapeDtypeStruct((sketch, variables), f32),
                jax.ShapeDtypeStruct((sketch, sketch), f32),
            ),
            in_specs=[any_spec] * 6,
            out_specs=(vmem_spec, vmem_spec),
            scratch_shapes=[
                pltpu.VMEM((sketch, variables), bf),
                pltpu.VMEM((rows, variables), bf),
                pltpu.VMEM((1, variables), f32),
                pltpu.VMEM((np_, LANES), f32),
                pltpu.VMEM((np_, LANES), i32),
                pltpu.VMEM((np_, LANES), i32),
                pltpu.VMEM((g, np_, 2, sketch // 2, LANES), bf),
                pltpu.VMEM((g, ng, sketch // 2, LANES), bf),
                pltpu.VMEM((g, nh, sketch // 2, LANES), bf),
                pltpu.VMEM((g, ng, sketch // 2, LANES), bf),
                cross, cross, cross, cross,
                pltpu.VMEM((g, ng, sketch // 2, LANES), bf),
                pltpu.VMEM((g, nh, sketch // 2, LANES), bf),
                dma((5,)),
                dma((ny,)),
                pltpu.SemaphoreType.REGULAR((3, 2)),
                per_g, per_g, per_h, per_h, per_g, per_g, per_x, per_x, per_x, per_x,
                gram_by_g, gram_by_g, gram_by_h, gram_by_h,
            ],
            compiler_params=pltpu.CompilerParams(collective_id=0, has_side_effects=True),
        )(
            omega,
            a_matrix,
            col_scale.reshape(1, variables),
            cone_point.reshape(np_, LANES),
            cone_id.reshape(np_, LANES),
            cone_kind.reshape(np_, LANES),
        )
    )


def solution(mesh):
    shape = mesh.shape
    parts = (4, 16, 2) if shape["col"] == 128 else (1, shape["col"], 1)
    split = Mesh(mesh.devices.reshape(shape["row"], *parts), ("row",) + COL)
    in_specs = (P("row", COL), P(None, COL), P(COL), P("row"), P("row"), P("row"))
    out_specs = (P(None, COL), P())
    return jax.shard_map(local, mesh=split, in_specs=in_specs, out_specs=out_specs, check_vma=False)
```

time: 94.4 us -> 87.3 us (0.925); the launches traced: 94.3 us -> 85.6 us
  Pallas kernels: 91.4 us -> 82.7 us
    pallas_call x1, Pallas kernels: 91.4 us -> 82.7 us  [local(): pl.pallas_call(body, out_shape=(jax.ShapeDtypeStruct((sketch, variables),...]
where the time goes in v3:
time: 87.3 us; the launch traced here: 85.6 us
  Pallas kernels  82.7 us (95%)
  local copies, waits for them, and re-layouts  2.25 us (3%)
    pallas_call x1, Pallas kernels, local(): pl.pallas_call(body, out_shape=(jax.ShapeDtypeStruct((sketch, variables),...  82.7 us
    unnamed x4, local copies, waits for them, and re-layouts  2.25 us

profile of v3, /device:TPU:1, one launch (start us, length us, event | category | flops | bytes accessed | tf_op | source)
XLA Modules:
  0.0 85.6 jit_solution(11090872507656002303)
XLA Ops:
  0.6 82.7 %shard_map.77 = (f32[96,512]{1,0:T(8,128)}, f32[96,96]{1,0:T(8,128)}) custom-call(bf16[96,512]{1,0:T(8,128)(2,1)} %refs_0_.1, bf16[1024,512]{1,0:T(8,128)(2,1)} %refs_1_.1, f32[1,512]{1,0:T(1,128)} %bitcast.7, f32[8,128]{1,0:T(8,128)} %bitcast.4, s32[8,128]{1,0:T(8,128)} %bitcast.5, s32[8,128]{1,0:T(8,128)} %bitcast.6), custom_call_target="tpu_custom_call" | custom-call | tf_op jit(solution)/shard_map/pallas_call | solution.py:477
  83.4 0.0 copy-start
  83.4 1.6 %copy.10 = f32[96,512]{1,0:T(8,128)} copy(f32[96,512]{1,0:T(8,128)} %get-tuple-element.4) | data formatting | bytes 393216
  85.0 0.0 copy-done
  85.0 0.6 copy.11
Async XLA Ops:
  83.4 1.6 %copy-start = (f32[96,96]{1,0:T(8,128)S(1)}, f32[96,96]{1,0:T(8,128)}, u32[]{:S(2)}) copy-start(f32[96,96]{1,0:T(8,128)} %get-tuple-element.5) | copy-start | bytes 110596

commit v4 on v3

--- a/solution.py
+++ b/solution.py
@@ -59,8 +59,8 @@
                 mult = {i: cols[t][i] * inv for i in cols[t]}
                 pivot = jnp.where(here, 1.0, rows[t])
                 for u in range(t + 1, step):
-                    rows[u] = jnp.where(here, 0.0, rows[u]) - down(mult[jb], s0 + u) * pivot
-                    head = down(cols[u][jb], s0 + t)
+                    head = down(cols[t][jb], s0 + u)
+                    rows[u] = jnp.where(here, 0.0, rows[u]) - head * inv * pivot
                     cols[u] = {i: cols[u][i] - mult[i] * head for i in cols[u]}
                 mults.append(mult)
                 pivots.append(jnp.where((lane > j + t) & (lane < j + step), 0.0, pivot))
@@ -477,8 +477,8 @@
         pl.pallas_call(
             body,
             out_shape=(
-                jax.ShapeDtypeStruct((sketch, variables), f32),
-                jax.ShapeDtypeStruct((sketch, sketch), f32),
+                pltpu.VMEM((sketch, variables), f32),
+                pltpu.VMEM((sketch, sketch), f32),
             ),
             in_specs=[any_spec] * 6,
             out_specs=(vmem_spec, vmem_spec),

time: 87.3 us -> 85.3 us (0.977)
  Pallas kernels: 82.7 us -> 81.7 us
  local copies, waits for them, and re-layouts: 2.25 us -> 1.3 us
    pallas_call x1, Pallas kernels: 82.7 us -> 81.7 us  [local(): pl.pallas_call(body, out_shape=(pltpu.VMEM((sketch, variables), f32), plt...]
    unnamed x4 -> x2, local copies, waits for them, and re-layouts: 2.25 us -> 1.3 us
where the time goes in v4:
time: 85.3 us; the launch traced here: 83.6 us
  Pallas kernels  81.7 us (96%)
  local copies, waits for them, and re-layouts  1.3 us (2%)
    pallas_call x1, Pallas kernels, local(): pl.pallas_call(body, out_shape=(pltpu.VMEM((sketch, variables), f32), plt...  81.7 us

profile of v4, /device:TPU:1, one launch (start us, length us, event | category | flops | bytes accessed | tf_op | source)
XLA Modules:
  0.0 83.6 jit_solution(980287539599604963)
XLA Ops:
  0.6 81.7 %shard_map.77 = (f32[96,512]{1,0:T(8,128)S(1)}, f32[96,96]{1,0:T(8,128)S(1)}) custom-call(bf16[96,512]{1,0:T(8,128)(2,1)} %refs_0_.1, bf16[1024,512]{1,0:T(8,128)(2,1)} %refs_1_.1, f32[1,512]{1,0:T(1,128)} %bitcast.7, f32[8,128]{1,0:T(8,128)} %bitcast.4, s32[8,128]{1,0:T(8,128)} %bitcast.5, s32[8,128]{1,0:T(8,128)} %bitcast.6), custom_call_target="tpu_custom_call" | custom-call | tf_op jit(solution)/shard_map/pallas_call | solution.py:477
  82.3 0.7 copy.10
  83.0 0.6 copy.11
